TPU v7x, 32 devices: a whole 2x2x4 slice. The times are simulated.
32 devices in a mesh: dp: 8 (over y, x, core), mp: 4 (over z).
Axes of the slice: x: 2, y: 2, z: 4, core: 2. Of those that a mesh axis runs over, the one named last changes fastest.
Arguments:
- tokens: bfloat16 [64, 256, 1024], P(('dp', 'mp')), may hold values from -6 to 6
- cotangent: bfloat16 [64, 256, 1024], P(('dp', 'mp')), may hold values from -6 to 6
- w_qkv: bfloat16 [3, 1024, 1024], P(None, None, 'mp'), may hold values from -0.1875 to 0.1875
- w_out: bfloat16 [1024, 1024], P('mp'), may hold values from -1 to 1
- w_up: bfloat16 [1024, 4096], P(None, 'mp'), may hold values from -0.1875 to 0.1875
- w_down: bfloat16 [4096, 1024], P('mp'), may hold values from -0.09375 to 0.09375
- w_mod: bfloat16 [1024, 6144], P('mp'), may hold values from -0.1875 to 0.1875
- b_mod: bfloat16 [6, 1024], replicated, may hold values from -3 to 3
- time_weight: bfloat16 [256, 1024], P(None, 'mp'), may hold values from -0.375 to 0.375
- class_table: bfloat16 [1000, 1024], P(None, 'mp'), may hold values from -6 to 6
- rel_table: bfloat16 [16, 961], P('mp'), may hold values from -5 to 5
- window_step: int32 [64], P('dp'), may hold values from 0 to 999
- window_label: int32 [64], P('dp'), may hold values from 0 to 999
- window_cols: int32 [64], P('dp'), may hold values from 0 to 16, as said below
Outputs:
- block_out: bfloat16 [64, 256, 1024], P(('dp', 'mp'))
- tokens_grad: bfloat16 [64, 256, 1024], P(('dp', 'mp'))
- w_qkv_grad: float32 [3, 1024, 1024], P(None, None, 'mp')
- w_out_grad: float32 [1024, 1024], P('mp')
- w_up_grad: float32 [1024, 4096], P(None, 'mp')
- w_down_grad: float32 [4096, 1024], P('mp')
- w_mod_grad: float32 [1024, 6144], P('mp')
- b_mod_grad: float32 [6, 1024], replicated
- time_weight_grad: float32 [256, 1024], P(None, 'mp')
- class_table_grad: float32 [1000, 1024], P(None, 'mp')
- rel_table_grad: float32 [16, 961], P('mp')
Inputs may be any that keep to these rules, and one draw needn't show every extreme that they name: `window_cols`: within each aligned block of 8 windows the used slots (nonzero entry) come first, two or more of them; some block is used in full. A used slot holds 16 or 8 valid columns, an unused one 0.
All inputs are finite; a program needn't handle non-finite values.
Results may differ from a plain program's by a relative error of at most 0.028.
Values may be sent and summed in bfloat16 or wider, within the bound.
No kernel may reach another device: no remote copies, remote signals or barrier semaphores. Data moves between devices by JAX's collectives and lax.ppermute only.
A program may use at most 192 MiB of HBM per device.

v0:
```python
import math
import jax
import jax.numpy as jnp
from jax import lax
from jax.sharding import PartitionSpec as P

HEAD_DIM = 64
WSIDE = 16
FREQ = 256
EPS = 1e-06
HIGH = lax.Precision.HIGHEST
MASKED = -1000000000.0


def exact(matrix_a, matrix_b):
    return jnp.dot(matrix_a, matrix_b, precision=HIGH, preferred_element_type=jnp.float32)


def layer_norm(field):
    center = field - jnp.mean(field, axis=-1, keepdims=True)
    spread = jnp.mean(center * center, axis=-1, keepdims=True)
    return center * lax.rsqrt(spread + EPS)


def modulate(field, scale_part, shift_part):
    return layer_norm(field) * (1.0 + scale_part) + shift_part


def gelu_tanh(field):
    return jax.nn.gelu(field, approximate=True)


def step_features(step_ids, half_width):
    frequency = jnp.exp(-math.log(10000.0) * jnp.arange(half_width, dtype=jnp.float32) / half_width)
    angles = step_ids.astype(jnp.float32)[:, None] * frequency[None, :]
    return jnp.concatenate([jnp.cos(angles), jnp.sin(angles)], axis=1)


def offset_table(window_side):
    offsets = jnp.arange(window_side, dtype=jnp.int32)
    offset_diff = offsets[:, None] - offsets[None, :] + window_side - 1
    return (
        offset_diff[None] == jnp.arange(2 * window_side - 1, dtype=jnp.int32)[:, None, None]
    ).astype(jnp.float32)


def make_scores(queries, keys, rel_bias, keep_keys, score_scale):
    raw_scores = (
        jnp.einsum("wihd,wjhd->whij", queries, keys, preferred_element_type=jnp.float32)
        * score_scale
        + rel_bias[None]
    )
    return jnp.where(keep_keys[:, None, None, :], raw_scores, MASKED)


def per_device(
    tokens,
    cotangent,
    w_qkv,
    w_out,
    w_up,
    w_down,
    w_mod,
    b_mod,
    time_weight,
    class_table,
    rel_table,
    window_step,
    window_label,
    window_cols,
):
    own_count, win_tok, width = tokens.shape
    group_size = window_step.shape[0]
    local_heads = w_out.shape[0] // HEAD_DIM
    score_scale = HEAD_DIM ** (-0.5)
    first_own = lax.axis_index("mp") * own_count
    features = step_features(window_step, FREQ // 2).astype(jnp.bfloat16)
    classes = jnp.arange(class_table.shape[0], dtype=jnp.int32)
    onehot = (window_label[:, None] == classes[None, :]).astype(jnp.bfloat16)
    cond_pre = jnp.dot(features, time_weight, preferred_element_type=jnp.float32) + jnp.dot(
        onehot, class_table, preferred_element_type=jnp.float32
    )
    condition = jax.nn.silu(cond_pre).astype(jnp.bfloat16)
    partial_mod = jnp.dot(condition, w_mod, preferred_element_type=jnp.float32)
    modulation = (
        lax.psum(partial_mod, "mp").reshape(group_size, 6, width) + b_mod.astype(jnp.float32)[None]
    )
    own_mod = lax.dynamic_slice_in_dim(modulation, first_own, own_count, 0)
    shift_attn, scale_attn, gate_attn, shift_mlp, scale_mlp, gate_mlp = [
        own_mod[:, column][:, None, :] for column in range(6)
    ]
    token_cols = jnp.arange(win_tok, dtype=jnp.int32) % WSIDE
    keep_keys = token_cols[None, :] < window_cols[:, None]
    keep_rows = lax.dynamic_slice_in_dim(keep_keys, first_own, own_count, 0)[:, :, None]
    rel_span = 2 * WSIDE - 1
    offset_pick = offset_table(WSIDE)
    rel_grid = rel_table.astype(jnp.float32).reshape(local_heads, rel_span, rel_span)
    half_bias = jnp.einsum("ayz,hab->hyzb", offset_pick, rel_grid, precision=HIGH)
    rel_bias = jnp.einsum("hyzb,bxw->hyxzw", half_bias, offset_pick, precision=HIGH).reshape(
        local_heads, win_tok, win_tok
    )
    inputs = tokens.astype(jnp.float32)
    normed_attn = modulate(inputs, scale_attn, shift_attn).astype(jnp.bfloat16)
    gathered_attn = lax.all_gather(normed_attn, "mp", axis=0, tiled=True)
    projected = jnp.einsum(
        "wtd,kde->kwte", gathered_attn, w_qkv, preferred_element_type=jnp.float32
    ).astype(jnp.bfloat16)
    split_shape = (group_size, win_tok, local_heads, HEAD_DIM)
    queries = projected[0].reshape(split_shape)
    keys = projected[1].reshape(split_shape)
    values = projected[2].reshape(split_shape)
    scores = make_scores(queries, keys, rel_bias, keep_keys, score_scale)
    row_max = jnp.max(scores, axis=-1, keepdims=True)
    log_total = row_max + jnp.log(jnp.sum(jnp.exp(scores - row_max), axis=-1, keepdims=True))
    probs_low = jnp.exp(scores - log_total).astype(jnp.bfloat16)
    attended = (
        jnp.einsum("whij,wjhd->wihd", probs_low, values, preferred_element_type=jnp.float32)
        .astype(jnp.bfloat16)
        .reshape(group_size, win_tok, local_heads * HEAD_DIM)
    )
    row_block = attended
    branch = lax.psum_scatter(
        jnp.einsum("wte,ed->wtd", row_block, w_out, preferred_element_type=jnp.float32).astype(
            jnp.bfloat16
        ),
        "mp",
        scatter_dimension=0,
        tiled=True,
    ).astype(jnp.float32)
    middle = inputs + gate_attn * branch
    normed_mlp = modulate(middle, scale_mlp, shift_mlp).astype(jnp.bfloat16)
    gathered_mlp = lax.all_gather(normed_mlp, "mp", axis=0, tiled=True)
    hidden_pre = jnp.einsum("wtd,df->wtf", gathered_mlp, w_up, preferred_element_type=jnp.float32)
    activation = gelu_tanh(hidden_pre).astype(jnp.bfloat16)
    row_block = activation
    mlp_out = lax.psum_scatter(
        jnp.einsum("wtf,fd->wtd", row_block, w_down, preferred_element_type=jnp.float32).astype(
            jnp.bfloat16
        ),
        "mp",
        scatter_dimension=0,
        tiled=True,
    ).astype(jnp.float32)
    block_out = jnp.where(keep_rows, middle + gate_mlp * mlp_out, 0.0).astype(jnp.bfloat16)
    grad_rows = jnp.where(keep_rows, cotangent.astype(jnp.float32), 0.0)
    d_gate_mlp = jnp.sum(grad_rows * mlp_out, axis=1)
    d_mlp = (gate_mlp * grad_rows).astype(jnp.bfloat16)
    d_mlp_all = lax.all_gather(d_mlp, "mp", axis=0, tiled=True)
    normed_again = lax.all_gather(normed_mlp, "mp", axis=0, tiled=True)
    pre_again = jnp.einsum("wtd,df->wtf", normed_again, w_up, preferred_element_type=jnp.float32)
    act_again = gelu_tanh(pre_again).astype(jnp.bfloat16)
    w_down_grad = jnp.einsum(
        "wtf,wtd->fd", act_again, d_mlp_all, preferred_element_type=jnp.float32
    )
    d_act = jnp.einsum("wtd,fd->wtf", d_mlp_all, w_down, preferred_element_type=jnp.float32)
    d_hidden = jax.vjp(gelu_tanh, pre_again)[1](d_act)[0].astype(jnp.bfloat16)
    w_up_grad = jnp.einsum(
        "wtd,wtf->df", normed_again, d_hidden, preferred_element_type=jnp.float32
    )
    row_block = d_hidden
    d_normed_mlp = lax.psum_scatter(
        jnp.einsum("wtf,df->wtd", row_block, w_up, preferred_element_type=jnp.float32),
        "mp",
        scatter_dimension=0,
        tiled=True,
    )
    pull_mlp = jax.vjp(modulate, middle, scale_mlp, shift_mlp)[1]
    d_middle_norm, d_scale_mlp, d_shift_mlp = pull_mlp(d_normed_mlp)
    d_middle = grad_rows + d_middle_norm
    d_gate_attn = jnp.sum(d_middle * branch, axis=1)
    d_branch = (gate_attn * d_middle).astype(jnp.bfloat16)
    d_branch_all = lax.all_gather(d_branch, "mp", axis=0, tiled=True)
    w_out_grad = jnp.einsum(
        "wte,wtd->ed", attended, d_branch_all, preferred_element_type=jnp.float32
    )
    d_attended = (
        jnp.einsum("wtd,ed->wte", d_branch_all, w_out, preferred_element_type=jnp.float32)
        .astype(jnp.bfloat16)
        .reshape(split_shape)
    )
    probs_back = jnp.exp(make_scores(queries, keys, rel_bias, keep_keys, score_scale) - log_total)
    d_probs = jnp.einsum("wihd,wjhd->whij", d_attended, values, preferred_element_type=jnp.float32)
    d_values = jnp.einsum(
        "whij,wihd->wjhd",
        probs_back.astype(jnp.bfloat16),
        d_attended,
        preferred_element_type=jnp.float32,
    ).astype(jnp.bfloat16)
    row_delta = jnp.sum(probs_back * d_probs, axis=-1, keepdims=True)
    d_scores = (probs_back * (d_probs - row_delta)).astype(jnp.bfloat16)
    d_queries = (
        jnp.einsum("whij,wjhd->wihd", d_scores, keys, preferred_element_type=jnp.float32)
        * score_scale
    ).astype(jnp.bfloat16)
    d_keys = (
        jnp.einsum("whij,wihd->wjhd", d_scores, queries, preferred_element_type=jnp.float32)
        * score_scale
    ).astype(jnp.bfloat16)
    d_bias = jnp.sum(d_scores, axis=0, dtype=jnp.float32).reshape(
        local_heads, WSIDE, WSIDE, WSIDE, WSIDE
    )
    d_half = jnp.einsum("hyxzw,bxw->hyzb", d_bias, offset_pick, precision=HIGH)
    rel_table_grad = jnp.einsum("hyzb,ayz->hab", d_half, offset_pick, precision=HIGH).reshape(
        local_heads, rel_span * rel_span
    )
    d_projected = jnp.stack([d_queries, d_keys, d_values]).reshape(
        3, group_size, win_tok, local_heads * HEAD_DIM
    )
    w_qkv_grad = jnp.einsum(
        "wtd,kwte->kde", gathered_attn, d_projected, preferred_element_type=jnp.float32
    )
    row_block = d_projected
    d_normed_attn = lax.psum_scatter(
        jnp.einsum("kwte,kde->wtd", row_block, w_qkv, preferred_element_type=jnp.float32).astype(
            jnp.bfloat16
        ),
        "mp",
        scatter_dimension=0,
        tiled=True,
    ).astype(jnp.float32)
    pull_attn = jax.vjp(modulate, inputs, scale_attn, shift_attn)[1]
    d_inputs_norm, d_scale_attn, d_shift_attn = pull_attn(d_normed_attn)
    tokens_grad = (d_middle + d_inputs_norm).astype(jnp.bfloat16)
    d_mod_own = jnp.stack(
        [
            d_shift_attn[:, 0],
            d_scale_attn[:, 0],
            d_gate_attn,
            d_shift_mlp[:, 0],
            d_scale_mlp[:, 0],
            d_gate_mlp,
        ],
        axis=1,
    ).reshape(own_count, 6 * width)
    d_modulation = lax.all_gather(d_mod_own.astype(jnp.bfloat16), "mp", axis=0, tiled=True).astype(
        d_mod_own.dtype
    )
    d_condition = exact(d_modulation, w_mod.T)
    d_cond_pre = jax.vjp(jax.nn.silu, cond_pre)[1](d_condition)[0]
    time_weight_grad = exact(features.astype(jnp.float32).T, d_cond_pre)
    class_table_grad = exact(onehot.astype(jnp.float32).T, d_cond_pre)
    w_mod_grad = exact(condition.astype(jnp.float32).T, d_modulation)
    b_mod_grad = jnp.sum(d_modulation, axis=0).reshape(6, width)
    (
        w_qkv_grad,
        w_out_grad,
        w_up_grad,
        w_down_grad,
        w_mod_grad,
        b_mod_grad,
        time_weight_grad,
        class_table_grad,
        rel_table_grad,
    ) = lax.psum(
        (
            w_qkv_grad,
            w_out_grad,
            w_up_grad,
            w_down_grad,
            w_mod_grad,
            b_mod_grad,
            time_weight_grad,
            class_table_grad,
            rel_table_grad,
        ),
        "dp",
    )
    return (
        block_out,
        tokens_grad,
        w_qkv_grad,
        w_out_grad,
        w_up_grad,
        w_down_grad,
        w_mod_grad,
        b_mod_grad,
        time_weight_grad,
        class_table_grad,
        rel_table_grad,
    )


def solution(mesh):
    return jax.shard_map(
        per_device,
        mesh=mesh,
        in_specs=(
            P(("dp", "mp"), None, None),
            P(("dp", "mp"), None, None),
            P(None, None, "mp"),
            P("mp", None),
            P(None, "mp"),
            P("mp", None),
            P("mp", None),
            P(),
            P(None, "mp"),
            P(None, "mp"),
            P("mp", None),
            P("dp"),
            P("dp"),
            P("dp"),
        ),
        out_specs=(
            P(("dp", "mp"), None, None),
            P(("dp", "mp"), None, None),
            P(None, None, "mp"),
            P("mp", None),
            P(None, "mp"),
            P("mp", None),
            P("mp", None),
            P(),
            P(None, "mp"),
            P(None, "mp"),
            P("mp", None),
        ),
        check_vma=False,
    )
```

profile of v0, /device:TPU:0, one launch (start us, length us, event | category | flops | bytes accessed | tf_op | source)
XLA Modules:
  0.0 1149.7 jit_solution(5632088591709699951)
XLA Ops:
  14.9 34.8 %all-reduce.5.cloned.1.call-done = f32[8,6,1024]{2,0,1:T(8,128)} async-done(((f32[8,6,1024]{2,0,1:T(8,128)}), f32[8,6,1024]{2,0,1:T(8,128)}) %all-reduce.5.cloned.1.call-update) | async-done | bytes 196624 | tf_op jit(solution)/shard_map/psum | solution.py:86
  54.1 5.6 convolution_bitcast_fusion
  59.8 12.0 %copy.103 = f32[4,16,16,16,16]{2,1,4,3,0:T(8,128)} copy(f32[4,16,16,16,16]{3,4,1,0,2:T(8,128)} %convolution_bitcast_fusion) | data formatting | bytes 2097152 | tf_op jit(solution)/shard_map/add | solution.py:49
  71.8 7.0 reshape.213
  78.9 55.0 %all-gather.6.cloned.1.call-done = bf16[8,256,1024]{2,1,0:T(8,128)(2,1)} async-done(((bf16[2,256,1024]{2,1,0:T(8,128)(2,1)}), bf16[8,256,1024]{2,1,0:T(8,128)(2,1)}) %all-gather.6.cloned.1.call-update) | async-done | bytes 4194320 | tf_op jit(solution)/shard_map/all_gather | solution.py:104
  133.9 6.1 convert_bitcast_fusion
  153.3 75.4 %reduce-scatter.5.cloned.1.call-done = bf16[2,256,1024]{2,1,0:T(8,128)(2,1)} async-done(((bf16[8,256,1024]{2,1,0:T(8,128)(2,1)}), bf16[2,256,1024]{2,1,0:T(8,128)(2,1)}) %reduce-scatter.5.cloned.1.call-update) | async-done | bytes 1048592 | tf_op jit(solution)/shard_map/reduce_scatter | solution.py:122
  237.2 78.7 %all-gather.8.cloned.1.call-done = bf16[8,256,1024]{2,1,0:T(8,128)(2,1)} async-done(((bf16[2,256,1024]{2,1,0:T(8,128)(2,1)}), bf16[8,256,1024]{2,1,0:T(8,128)(2,1)}) %all-gather.8.cloned.1.call-update) | async-done | bytes 4194320 | tf_op jit(solution)/shard_map/all_gather | solution.py:132
  316.0 10.9 fusion.34
  326.9 70.4 %all-gather.10.cloned.1.call-done = bf16[8,256,1024]{2,1,0:T(8,128)(2,1)} async-done(((bf16[2,256,1024]{2,1,0:T(8,128)(2,1)}), bf16[8,256,1024]{2,1,0:T(8,128)(2,1)}) %all-gather.10.cloned.1.call-update) | async-done | bytes 4194320 | tf_op jit(solution)/shard_map/all_gather | solution.py:148
  397.2 12.8 %fusion.6 = bf16[8,256,1024]{2,1,0:T(8,128)(2,1)S(1)} fusion(f32[8,256,1024]{2,1,0:T(8,128)} %fusion.34, bf16[8,256,1024]{2,1,0:T(8,128)(2,1)} %all-gather.10.cloned.1.call-done, bf16[1024,1024]{1,0:T(8,128)(2,1)} %param.19), kind=kOutput, calls=%fused_computation.8 | convolution fusion | flops 4336910336 | bytes 18874368 | tf_op jit(solution)/shard_map/wtd,fd->wtf/dot_general | solution.py:155
  412.0 7.0 fusion.32
  419.1 143.2 %reduce-scatter.9.cloned.1.call-done = f32[2,256,1024]{2,1,0:T(8,128)} async-done(((f32[8,256,1024]{2,1,0:T(8,128)}), f32[2,256,1024]{2,1,0:T(8,128)}) %reduce-scatter.9.cloned.1.call-update) | async-done | bytes 2097168 | tf_op jit(solution)/shard_map/reduce_scatter | solution.py:161
  569.6 81.5 %all-gather.12.cloned.1.call-done = bf16[8,256,1024]{2,1,0:T(8,128)(2,1)} async-done(((bf16[2,256,1024]{2,1,0:T(8,128)(2,1)}), bf16[8,256,1024]{2,1,0:T(8,128)(2,1)}) %all-gather.12.cloned.1.call-update) | async-done | bytes 4194320 | tf_op jit(solution)/shard_map/all_gather | solution.py:172
  651.0 3.7 convolution_convert_fusion.3
  654.8 6.0 convolution_convert_fusion.2
  663.3 3.9 convert_reduce_fusion
  678.1 7.8 bitcast_convert_fusion
  686.0 11.5 %convolution_convert_fusion = bf16[8,256,1024]{2,1,0:T(8,128)(2,1)} fusion(bf16[1024,1024]{1,0:T(8,128)(2,1)} %param.19, f32[8,256,1024]{2,1,0:T(8,128)} %fusion.34), kind=kOutput, calls=%fused_computation.34 | convolution fusion | flops 4315938816 | bytes 14680064 | tf_op jit(solution)/shard_map/wtf,fd->wtd/dot_general | solution.py:137
  697.8 10.2 convolution_bitcast_fusion.2
  708.1 11.2 convolution_bitcast_fusion.1
  722.8 5.5 fusion.36
  728.3 33.1 %reduce-scatter.11.cloned.1.call-done = bf16[2,256,1024]{2,1,0:T(8,128)(2,1)} async-done(((bf16[8,256,1024]{2,1,0:T(8,128)(2,1)}), bf16[2,256,1024]{2,1,0:T(8,128)(2,1)}) %reduce-scatter.11.cloned.1.call-update) | async-done | bytes 1048592 | tf_op jit(solution)/shard_map/reduce_scatter | solution.py:213
  767.7 74.0 %reduce-scatter.7.cloned.1.call-done = bf16[2,256,1024]{2,1,0:T(8,128)(2,1)} async-done(((bf16[8,256,1024]{2,1,0:T(8,128)(2,1)}), bf16[2,256,1024]{2,1,0:T(8,128)(2,1)}) %reduce-scatter.7.cloned.1.call-update) | async-done | bytes 1048592 | tf_op jit(solution)/shard_map/reduce_scatter | solution.py:136
  841.6 5.2 fusion.26
  847.0 13.8 %all-gather = bf16[4,2,6144]{2,1,0:T(2,128)(2,1)S(1)} all-gather(bf16[1,2,6144]{2,1,0:T(2,128)(2,1)S(1)} %bitcast.178), channel_id=1, replica_groups=mesh['dp'=8,'mp'=4] {'mp'}, dimensions={0}, use_global_device_ids=true | all-gather | bytes 122880 | tf_op jit(solution)/shard_map/all_gather | solution.py:235
  864.4 3.7 fusion.77
  869.0 6.2 reshape.189
  875.2 6.8 convolution_bitcast_fusion.5
  882.7 25.6 %all-reduce = (f32[6,1024]{1,0:T(8,128)}, f32[4,961]{1,0:T(4,128)}) all-reduce(f32[6,1024]{1,0:T(8,128)S(1)} %reshape.188, f32[4,961]{1,0:T(4,128)S(1)} %reshape.190), channel_id=1, replica_groups=mesh['dp'=8,'mp'=4] {'dp'}, use_global_device_ids=true, to_apply=%region_28.29 | all-reduce | flops 9988 | bytes 79904 | tf_op jit(solution)/shard_map/psum | solution.py:254
  908.3 215.6 %all-reduce.7.cloned.1.call-done = (f32[3,1024,256]{1,2,0:T(8,128)}, f32[256,1024]{1,0:T(8,128)}, f32[1024,1024]{1,0:T(8,128)}, f32[1024,1024]{1,0:T(8,128)}, f3...) async-done(((f32[3,1024,256]{1,2,0:T(8,128)}, f32[256,1024]{1,0:T(8,128)}, f32[1024,1024]{1,0:T(8,128)}, f32[1024,1024]{1,0:T(8,128)}, ...) | async-done | bytes 20160528 | tf_op jit(solution)/shard_map/psum | solution.py:254
  1129.7 5.1 copy.125
  (172 shorter events, 85.5 us)
Async XLA Ops:
  7.2 42.5 %all-reduce.5.cloned.1.call-start = ((), (), s32[]{:S(2)}) async-start(), calls=%async_computation.4 | async-start | bytes 393216 | tf_op jit(solution)/shard_map/psum | solution.py:86
  8.2 6.7 copy-start.27
  11.7 41.7 %copy-start.28 = (bf16[4,961]{1,0:T(4,128)(2,1)S(1)}, bf16[4,961]{1,0:T(4,128)(2,1)}, u32[]{:S(2)}) copy-start(bf16[4,961]{1,0:T(4,128)(2,1)} %param.24) | copy-start | bytes 23068
  11.7 122.2 %all-gather.6.cloned.1.call-start = ((), (), s32[]{:S(2)}) async-start(), calls=%async_computation.5 | async-start | bytes 5242880 | tf_op jit(solution)/shard_map/all_gather | solution.py:104
  53.3 175.4 %reduce-scatter.5.cloned.1.call-start = ((), (), s32[]{:S(2)}) async-start(), calls=%async_computation.6 | async-start | bytes 5242880 | tf_op jit(solution)/shard_map/reduce_scatter | solution.py:122
  71.8 7.0 copy-start.30
  140.3 4.0 copy-start.7
  140.3 4.0 copy-start.12
  140.3 5.7 copy-start.9
  153.3 162.7 %all-gather.8.cloned.1.call-start = ((), (), s32[]{:S(2)}) async-start(), calls=%async_computation.7 | async-start | bytes 5242880 | tf_op jit(solution)/shard_map/all_gather | solution.py:132
  228.7 4.2 copy-start.2
  228.7 4.2 copy-start.4
  234.6 162.6 %all-gather.10.cloned.1.call-start = ((), (), s32[]{:S(2)}) async-start(), calls=%async_computation.9 | async-start | bytes 5242880 | tf_op jit(solution)/shard_map/all_gather | solution.py:148
  237.2 325.1 %reduce-scatter.9.cloned.1.call-start = ((), (), s32[]{:S(2)}) async-start(), calls=%async_computation.10 | async-start | bytes 10485760 | tf_op jit(solution)/shard_map/reduce_scatter | solution.py:161
  397.2 14.8 %copy-start.34 = (bf16[1024,1024]{1,0:T(8,128)(2,1)S(1)}, bf16[1024,1024]{1,0:T(8,128)(2,1)}, u32[]{:S(2)}) copy-start(bf16[1024,1024]{1,0:T(8,128)(2,1)} %param.18) | copy-start | bytes 6291460
  419.0 232.0 %all-gather.12.cloned.1.call-start = ((), (), s32[]{:S(2)}) async-start(), calls=%async_computation.11 | async-start | bytes 5242880 | tf_op jit(solution)/shard_map/all_gather | solution.py:172
  562.3 3.5 copy-start.14
  569.5 191.9 %reduce-scatter.11.cloned.1.call-start = ((), (), s32[]{:S(2)}) async-start(), calls=%async_computation.12 | async-start | bytes 5242880 | tf_op jit(solution)/shard_map/reduce_scatter | solution.py:213
  651.0 9.7 slice-start
  654.8 6.0 slice-start.1
  654.8 6.0 copy-start.10
  663.3 3.9 copy-start.13
  686.0 155.7 %reduce-scatter.7.cloned.1.call-start = ((), (), s32[]{:S(2)}) async-start(), calls=%async_computation.8 | async-start | bytes 5242880 | tf_op jit(solution)/shard_map/reduce_scatter | solution.py:136
  697.6 426.2 %all-reduce.7.cloned.1.call-start = ((), (), s32[]{:S(2)}) async-start(), calls=%async_computation.13 | async-start | bytes 40321024 | tf_op jit(solution)/shard_map/psum | solution.py:254
  697.8 10.2 copy-start.32
  708.1 11.2 copy-start.18
  708.1 11.2 copy-start.33
  719.3 3.6 copy-start.31
  846.9 15.9 %copy-start.29 = (s32[8]{0:T(128)S(1)}, s32[8]{0:T(128)}, u32[]{:S(2)}) copy-start(s32[8]{0:T(128)} %param.26) | copy-start | bytes 100
  1129.7 5.1 copy-start.16
  1129.7 7.2 slice-start.2
  1134.8 3.5 slice-start.3
  (18 other events, 40.4 us)
Sparse Core Ops, SparseCore 0:
  11.9 37.7 all-reduce.4
  53.5 80.3 all-gather.5
  153.4 75.2 reduce-scatter.4
  234.7 81.2 all-gather.7
  318.0 79.2 all-gather.9
  419.2 143.0 reduce-scatter.8
  569.6 81.3 all-gather.11
  686.1 75.2 reduce-scatter.10
  764.3 77.2 reduce-scatter.6
  868.3 255.4 all-reduce.6
where the time goes:
time: 1160 us; the launch traced here: 1150 us
  waiting for transfers between devices  862 us (74%)
  matrix products  133 us (11%)
  local copies, waits for them, and re-layouts  60.8 us (5%)
  blocking collectives  39.4 us (3%)
  other arithmetic  38.9 us (3%)
  between operations  14.9 us (1%)
    psum x1, waiting for transfers between devices, per_device(): lax.psum((w_qkv_grad, w_out_grad, w_up_grad, w_down_grad, w_mod_grad, b_m...  216 us
    reduce_scatter x1, waiting for transfers between devices, per_device(): lax.psum_scatter(jnp.einsum('wtf,df->wtd', row_block, w_up, preferred_ele...  143 us
    all_gather x1, waiting for transfers between devices, per_device(): d_branch_all = lax.all_gather(d_branch, 'mp', axis=0, tiled=True)  81.5 us
    all_gather x1, waiting for transfers between devices, per_device(): gathered_mlp = lax.all_gather(normed_mlp, 'mp', axis=0, tiled=True)  78.7 us
    reduce_scatter x1, waiting for transfers between devices, per_device(): lax.psum_scatter(jnp.einsum('wte,ed->wtd', row_block, w_out, preferred_el...  75.4 us
    reduce_scatter x1, waiting for transfers between devices, per_device(): lax.psum_scatter(jnp.einsum('wtf,fd->wtd', row_block, w_down, preferred_e...  74 us
    all_gather x1, waiting for transfers between devices, per_device(): d_mlp_all = lax.all_gather(d_mlp, 'mp', axis=0, tiled=True)  70.4 us
    all_gather x1, waiting for transfers between devices, per_device(): gathered_attn = lax.all_gather(normed_attn, 'mp', axis=0, tiled=True)  55 us
  transfers between devices with their start and end apart: 10, of which 10 were waited for; matrix products, arithmetic and copies ran while one was open for 9% of the time, Pallas kernels for 0%

commit v1 on v0

--- a/solution.py
+++ b/solution.py
@@ -101,7 +101,15 @@
     )
     inputs = tokens.astype(jnp.float32)
     normed_attn = modulate(inputs, scale_attn, shift_attn).astype(jnp.bfloat16)
-    gathered_attn = lax.all_gather(normed_attn, "mp", axis=0, tiled=True)
+    ways, here = (lax.axis_size("mp"), lax.axis_index("mp"))
+    grown, reach = (normed_attn, 1)
+    while reach < ways:
+        theirs = lax.ppermute(grown, "mp", [(d, d ^ reach) for d in range(ways)])
+        mine_first = jnp.concatenate([grown, theirs], axis=0)
+        theirs_first = jnp.concatenate([theirs, grown], axis=0)
+        grown = jnp.where(here & reach == 0, mine_first, theirs_first)
+        reach = 2 * reach
+    gathered_attn = grown
     projected = jnp.einsum(
         "wtd,kde->kwte", gathered_attn, w_qkv, preferred_element_type=jnp.float32
     ).astype(jnp.bfloat16)

time: 1160 us -> 1200 us (1.034)
  waiting for transfers between devices: 862 us -> 890 us
    ppermute x0 -> x2, waiting for transfers between devices: none -> 84.6 us  [per_device(): theirs = lax.ppermute(grown, 'mp', [(d, d ^ reach) for d in range(ways)])]
    all_gather x1 -> x0, waiting for transfers between devices: 55 us -> none  [per_device(): gathered_attn = lax.all_gather(normed_attn, 'mp', axis=0, tiled=True)]
    unnamed x93 -> x111, local copies, waits for them, and re-layouts: 28.4 us -> 27.8 us
  transfers between devices with their start and end apart: 10 -> 11, of which waited for: 10 -> 11; matrix products, arithmetic and copies ran while one was open for 9% -> 9% of each run, Pallas kernels for 0% -> 0%
where the time goes in v1:
time: 1200 us; the launch traced here: 1190 us
  waiting for transfers between devices  890 us (74%)
  matrix products  138 us (12%)
  local copies, waits for them, and re-layouts  60.1 us (5%)
  other arithmetic  42.9 us (4%)
  blocking collectives  39.5 us (3%)
  between operations  14.8 us (1%)
    psum x1, waiting for transfers between devices, per_device(): lax.psum((w_qkv_grad, w_out_grad, w_up_grad, w_down_grad, w_mod_grad, b_m...  215 us
    reduce_scatter x1, waiting for transfers between devices, per_device(): lax.psum_scatter(jnp.einsum('wtf,df->wtd', row_block, w_up, preferred_ele...  143 us
    ppermute x2, waiting for transfers between devices, per_device(): theirs = lax.ppermute(grown, 'mp', [(d, d ^ reach) for d in range(ways)])  84.6 us
    all_gather x1, waiting for transfers between devices, per_device(): d_branch_all = lax.all_gather(d_branch, 'mp', axis=0, tiled=True)  81.5 us
    all_gather x1, waiting for transfers between devices, per_device(): gathered_mlp = lax.all_gather(normed_mlp, 'mp', axis=0, tiled=True)  78.8 us
    reduce_scatter x1, waiting for transfers between devices, per_device(): lax.psum_scatter(jnp.einsum('wte,ed->wtd', row_block, w_out, preferred_el...  76.9 us
    reduce_scatter x1, waiting for transfers between devices, per_device(): lax.psum_scatter(jnp.einsum('wtf,fd->wtd', row_block, w_down, preferred_e...  73.9 us
    all_gather x1, waiting for transfers between devices, per_device(): d_mlp_all = lax.all_gather(d_mlp, 'mp', axis=0, tiled=True)  70.4 us
  transfers between devices with their start and end apart: 11, of which 11 were waited for; matrix products, arithmetic and copies ran while one was open for 9% of the time, Pallas kernels for 0%

profile of v1, /device:TPU:0, one launch (start us, length us, event | category | flops | bytes accessed | tf_op | source)
XLA Modules:
  0.0 1189.9 jit_solution(5076066841870720347)
XLA Ops:
  15.6 34.7 %all-reduce.5.cloned.1.call-done = f32[8,6,1024]{2,0,1:T(8,128)} async-done(((f32[8,6,1024]{2,0,1:T(8,128)}), f32[8,6,1024]{2,0,1:T(8,128)}) %all-reduce.5.cloned.1.call-update) | async-done | bytes 196624 | tf_op jit(solution)/shard_map/psum | solution.py:86
  55.3 21.7 %collective-permute-done = bf16[2,256,1024]{2,1,0:T(8,128)(2,1)} collective-permute-done((bf16[2,256,1024]{2,1,0:T(8,128)(2,1)}, bf16[2,256,1024]{2,1,0:T(8,128)(2,1)}, u32[]{:S(2)}, u32[]{:S(2)}) %collective-permute-start) | collective-permute-done | bytes 1048608 | tf_op jit(solution)/shard_map/ppermute | solution.py:107
  77.0 3.9 maximum_select_fusion.1
  84.0 5.7 convolution_bitcast_fusion
  89.6 11.9 %copy.103 = f32[4,16,16,16,16]{2,1,4,3,0:T(8,128)} copy(f32[4,16,16,16,16]{3,4,1,0,2:T(8,128)} %convolution_bitcast_fusion) | data formatting | bytes 2097152 | tf_op jit(solution)/shard_map/add | solution.py:49
  101.5 6.9 reshape.213
  108.6 62.9 %collective-permute-done.1 = bf16[4,256,1024]{2,1,0:T(8,128)(2,1)} collective-permute-done((bf16[4,256,1024]{2,1,0:T(8,128)(2,1)}, bf16[4,256,1024]{2,1,0:T(8,128)(2,1)}, u32[]{:S(2)}, u32[]{:S(2)}) %collective-permute-start.1) | collective-permute-done | bytes 2097184 | tf_op jit(solution)/shard_map/ppermute | solution.py:107
  171.5 7.4 convert_bitcast_fusion
  192.1 76.9 %reduce-scatter.5.cloned.1.call-done = bf16[2,256,1024]{2,1,0:T(8,128)(2,1)} async-done(((bf16[8,256,1024]{2,1,0:T(8,128)(2,1)}), bf16[2,256,1024]{2,1,0:T(8,128)(2,1)}) %reduce-scatter.5.cloned.1.call-update) | async-done | bytes 1048592 | tf_op jit(solution)/shard_map/reduce_scatter | solution.py:130
  277.6 78.8 %all-gather.5.cloned.1.call-done = bf16[8,256,1024]{2,1,0:T(8,128)(2,1)} async-done(((bf16[2,256,1024]{2,1,0:T(8,128)(2,1)}), bf16[8,256,1024]{2,1,0:T(8,128)(2,1)}) %all-gather.5.cloned.1.call-update) | async-done | bytes 4194320 | tf_op jit(solution)/shard_map/all_gather | solution.py:140
  356.3 10.9 fusion.35
  367.2 70.4 %all-gather.7.cloned.1.call-done = bf16[8,256,1024]{2,1,0:T(8,128)(2,1)} async-done(((bf16[2,256,1024]{2,1,0:T(8,128)(2,1)}), bf16[8,256,1024]{2,1,0:T(8,128)(2,1)}) %all-gather.7.cloned.1.call-update) | async-done | bytes 4194320 | tf_op jit(solution)/shard_map/all_gather | solution.py:156
  437.6 12.7 %fusion.6 = bf16[8,256,1024]{2,1,0:T(8,128)(2,1)S(1)} fusion(f32[8,256,1024]{2,1,0:T(8,128)} %fusion.35, bf16[8,256,1024]{2,1,0:T(8,128)(2,1)} %all-gather.7.cloned.1.call-done, bf16[1024,1024]{1,0:T(8,128)(2,1)} %param.19), kind=kOutput, calls=%fused_computation.8 | convolution fusion | flops 4336910336 | bytes 18874368 | tf_op jit(solution)/shard_map/wtd,fd->wtf/dot_general | solution.py:163
  452.4 7.0 fusion.33
  459.4 143.2 %reduce-scatter.9.cloned.1.call-done = f32[2,256,1024]{2,1,0:T(8,128)} async-done(((f32[8,256,1024]{2,1,0:T(8,128)}), f32[2,256,1024]{2,1,0:T(8,128)}) %reduce-scatter.9.cloned.1.call-update) | async-done | bytes 2097168 | tf_op jit(solution)/shard_map/reduce_scatter | solution.py:169
  609.9 81.5 %all-gather.9.cloned.1.call-done = bf16[8,256,1024]{2,1,0:T(8,128)(2,1)} async-done(((bf16[2,256,1024]{2,1,0:T(8,128)(2,1)}), bf16[8,256,1024]{2,1,0:T(8,128)(2,1)}) %all-gather.9.cloned.1.call-update) | async-done | bytes 4194320 | tf_op jit(solution)/shard_map/all_gather | solution.py:180
  695.1 6.0 convolution_convert_fusion.2
  703.6 3.9 convert_reduce_fusion
  718.5 7.8 bitcast_convert_fusion
  726.4 11.5 convolution_convert_fusion
  738.2 10.2 convolution_bitcast_fusion.2
  748.4 11.2 convolution_bitcast_fusion.1
  761.9 8.9 fusion.37
  770.9 30.9 %reduce-scatter.11.cloned.1.call-done = bf16[2,256,1024]{2,1,0:T(8,128)(2,1)} async-done(((bf16[8,256,1024]{2,1,0:T(8,128)(2,1)}), bf16[2,256,1024]{2,1,0:T(8,128)(2,1)}) %reduce-scatter.11.cloned.1.call-update) | async-done | bytes 1048592 | tf_op jit(solution)/shard_map/reduce_scatter | solution.py:221
  808.1 73.9 %reduce-scatter.7.cloned.1.call-done = bf16[2,256,1024]{2,1,0:T(8,128)(2,1)} async-done(((bf16[8,256,1024]{2,1,0:T(8,128)(2,1)}), bf16[2,256,1024]{2,1,0:T(8,128)(2,1)}) %reduce-scatter.7.cloned.1.call-update) | async-done | bytes 1048592 | tf_op jit(solution)/shard_map/reduce_scatter | solution.py:144
  882.0 5.2 fusion.27
  887.3 13.8 %all-gather = bf16[4,2,6144]{2,1,0:T(2,128)(2,1)S(1)} all-gather(bf16[1,2,6144]{2,1,0:T(2,128)(2,1)S(1)} %bitcast.177), channel_id=1, replica_groups=mesh['dp'=8,'mp'=4] {'mp'}, dimensions={0}, use_global_device_ids=true | all-gather | bytes 122880 | tf_op jit(solution)/shard_map/all_gather | solution.py:243
  909.4 6.2 reshape.189
  915.6 6.8 convolution_bitcast_fusion.5
  923.1 25.7 %all-reduce = (f32[6,1024]{1,0:T(8,128)}, f32[4,961]{1,0:T(4,128)}) all-reduce(f32[6,1024]{1,0:T(8,128)S(1)} %reshape.188, f32[4,961]{1,0:T(4,128)S(1)} %reshape.190), channel_id=1, replica_groups=mesh['dp'=8,'mp'=4] {'dp'}, use_global_device_ids=true, to_apply=%region_28.29 | all-reduce | flops 9988 | bytes 79904 | tf_op jit(solution)/shard_map/psum | solution.py:262
  948.8 215.4 %all-reduce.7.cloned.1.call-done = (f32[3,1024,256]{1,2,0:T(8,128)}, f32[256,1024]{1,0:T(8,128)}, f32[1024,1024]{1,0:T(8,128)}, f32[1024,1024]{1,0:T(8,128)}, f3...) async-done(((f32[3,1024,256]{1,2,0:T(8,128)}, f32[256,1024]{1,0:T(8,128)}, f32[1024,1024]{1,0:T(8,128)}, f32[1024,1024]{1,0:T(8,128)}, ...) | async-done | bytes 20160528 | tf_op jit(solution)/shard_map/psum | solution.py:262
  1170.1 5.1 copy.125
  (192 shorter events, 96.0 us)
Async XLA Ops:
  7.2 43.1 %all-reduce.5.cloned.1.call-start = ((), (), s32[]{:S(2)}) async-start(), calls=%async_computation.4 | async-start | bytes 393216 | tf_op jit(solution)/shard_map/psum | solution.py:86
  8.2 7.3 copy-start.37
  12.4 256.7 %reduce-scatter.5.cloned.1.call-start = ((), (), s32[]{:S(2)}) async-start(), calls=%async_computation.5 | async-start | bytes 5242880 | tf_op jit(solution)/shard_map/reduce_scatter | solution.py:130
  15.5 34.8 %copy-start.35 = (f32[2,256]{1,0:T(2,128)}, f32[2,256]{1,0:T(2,128)S(1)}, u32[]{:S(2)}) copy-start(f32[2,256]{1,0:T(2,128)S(1)} %fusion.29) | copy-start | bytes 6148
  15.6 65.4 %copy-start.29 = (f32[2,256]{1,0:T(2,128)}, f32[2,256]{1,0:T(2,128)S(1)}, u32[]{:S(2)}) copy-start(f32[2,256]{1,0:T(2,128)S(1)} %fusion.72) | copy-start | bytes 6148
  51.3 31.9 %copy-start.38 = (bf16[4,961]{1,0:T(4,128)(2,1)S(1)}, bf16[4,961]{1,0:T(4,128)(2,1)}, u32[]{:S(2)}) copy-start(bf16[4,961]{1,0:T(4,128)(2,1)} %param.24) | copy-start | bytes 23068
  54.0 23.1 %collective-permute-start = (bf16[2,256,1024]{2,1,0:T(8,128)(2,1)}, bf16[2,256,1024]{2,1,0:T(8,128)(2,1)}, u32[]{:S(2)}, u32[]{:S(2)}) collective-permute-start(bf16[2,256,1024]{2,1,0:T(8,128)(2,1)} %fusion.22), channel_id=1, source_target_pairs={{0,1},{1,0},{2,3},{3,2},{4,5},{5,4},{6,7},{7,6},{8,9},{9,8},{10,11... | collective-permute-start | bytes 3145736 | tf_op jit(solution)/shard_map/ppermute | solution.py:107
  81.0 90.5 %collective-permute-start.1 = (bf16[4,256,1024]{2,1,0:T(8,128)(2,1)}, bf16[4,256,1024]{2,1,0:T(8,128)(2,1)}, u32[]{:S(2)}, u32[]{:S(2)}) collective-permute-start(bf16[4,256,1024]{2,1,0:T(8,128)(2,1)} %maximum_select_fusion.1), channel_id=1, source_target_pairs={{0,2},{1,3},{2,0},{3,1},{4,6},{5,7},{6,4},{7,5},{8,10},{9,11},{10,... | collective-permute-start | bytes 6291464 | tf_op jit(solution)/shard_map/ppermute | solution.py:107
  101.5 6.9 copy-start.40
  179.1 5.7 copy-start.9
  192.1 164.3 %all-gather.5.cloned.1.call-start = ((), (), s32[]{:S(2)}) async-start(), calls=%async_computation.6 | async-start | bytes 5242880 | tf_op jit(solution)/shard_map/all_gather | solution.py:140
  274.9 162.7 %all-gather.7.cloned.1.call-start = ((), (), s32[]{:S(2)}) async-start(), calls=%async_computation.8 | async-start | bytes 5242880 | tf_op jit(solution)/shard_map/all_gather | solution.py:156
  277.5 325.1 %reduce-scatter.9.cloned.1.call-start = ((), (), s32[]{:S(2)}) async-start(), calls=%async_computation.9 | async-start | bytes 10485760 | tf_op jit(solution)/shard_map/reduce_scatter | solution.py:169
  437.6 14.8 %copy-start.43 = (bf16[1024,1024]{1,0:T(8,128)(2,1)S(1)}, bf16[1024,1024]{1,0:T(8,128)(2,1)}, u32[]{:S(2)}) copy-start(bf16[1024,1024]{1,0:T(8,128)(2,1)} %param.18) | copy-start | bytes 6291460
  459.4 232.0 %all-gather.9.cloned.1.call-start = ((), (), s32[]{:S(2)}) async-start(), calls=%async_computation.10 | async-start | bytes 5242880 | tf_op jit(solution)/shard_map/all_gather | solution.py:180
  609.9 191.9 %reduce-scatter.11.cloned.1.call-start = ((), (), s32[]{:S(2)}) async-start(), calls=%async_computation.11 | async-start | bytes 5242880 | tf_op jit(solution)/shard_map/reduce_scatter | solution.py:221
  691.4 9.7 slice-start
  695.1 6.0 slice-start.1
  695.1 6.0 copy-start.10
  726.4 155.6 %reduce-scatter.7.cloned.1.call-start = ((), (), s32[]{:S(2)}) async-start(), calls=%async_computation.7 | async-start | bytes 5242880 | tf_op jit(solution)/shard_map/reduce_scatter | solution.py:144
  738.0 426.3 %all-reduce.7.cloned.1.call-start = ((), (), s32[]{:S(2)}) async-start(), calls=%async_computation.12 | async-start | bytes 40321024 | tf_op jit(solution)/shard_map/psum | solution.py:262
  738.2 10.2 copy-start.41
  748.4 11.2 copy-start.18
  748.4 11.2 copy-start.42
  770.9 34.5 %copy-start.36 = (f32[2,256]{1,0:T(2,128)S(1)}, f32[2,256]{1,0:T(2,128)}, u32[]{:S(2)}) copy-start(f32[2,256]{1,0:T(2,128)} %copy-done.35) | copy-start | bytes 6148
  770.9 34.5 %copy-start.30 = (f32[2,256]{1,0:T(2,128)S(1)}, f32[2,256]{1,0:T(2,128)}, u32[]{:S(2)}) copy-start(f32[2,256]{1,0:T(2,128)} %copy-done.29) | copy-start | bytes 6148
  887.2 14.9 %copy-start.28 = (f32[8,256]{1,0:T(8,128)S(1)}, f32[8,256]{1,0:T(8,128)}, u32[]{:S(2)}) copy-start(f32[8,256]{1,0:T(8,128)} %copy-done.27) | copy-start | bytes 24580
  887.2 14.9 %copy-start.32 = (bf16[8,128]{1,0:T(8,128)(2,1)S(1)}, bf16[8,128]{1,0:T(8,128)(2,1)}, u32[]{:S(2)}) copy-start(bf16[8,128]{1,0:T(8,128)(2,1)} %copy-done.31) | copy-start | bytes 6148
  887.2 14.9 %copy-start.34 = (bf16[8,128]{1,0:T(8,128)(2,1)S(1)}, bf16[8,128]{1,0:T(8,128)(2,1)}, u32[]{:S(2)}) copy-start(bf16[8,128]{1,0:T(8,128)(2,1)} %copy-done.33) | copy-start | bytes 6148
  887.3 15.9 %copy-start.39 = (s32[8]{0:T(128)S(1)}, s32[8]{0:T(128)}, u32[]{:S(2)}) copy-start(s32[8]{0:T(128)} %param.26) | copy-start | bytes 100
  1170.1 5.1 copy-start.16
  1170.1 7.2 slice-start.2
  (28 other events, 71.6 us)
Sparse Core Ops, SparseCore 0:
  12.5 37.7 all-reduce.4
  192.2 76.7 reduce-scatter.4
  275.0 81.2 all-gather.4
  358.3 79.2 all-gather.6
  459.5 143.0 reduce-scatter.8
  610.0 81.3 all-gather.8
  726.5 75.2 reduce-scatter.10
  804.7 77.2 reduce-scatter.6
  908.7 255.4 all-reduce.6
